TPU v7x, 32 devices: a whole 2x2x4 slice. The times are simulated.
32 devices in a mesh: dp: 4 (over z), row: 4 (over y, core), col: 2 (over x).
Axes of the slice: x: 2, y: 2, z: 4, core: 2. Of those that a mesh axis runs over, the one named last changes fastest.
Arguments:
- latents: bfloat16 [4096, 2048], P(('dp', 'col'), 'row'), parts along dimension 0, may hold values from -64 to 64
- norm_gain: float32 [8192], P(('dp', 'row')), parts along dimension 0, may hold values from 0.1 to 1.9
- q_weight: bfloat16 [8192, 2048], P(('dp', 'row'), 'col'), parts along dimension 0, may hold values from -1 to 1
- k_weight: bfloat16 [8192, 2048], P(('dp', 'row'), 'col'), parts along dimension 0, may hold values from -1 to 1
- v_weight: bfloat16 [8192, 2048], P(('dp', 'row'), 'col'), parts along dimension 0, may hold values from -0.125 to 0.125
- out_weight: bfloat16 [8192, 2048], P(('dp', 'col'), 'row'), parts along dimension 0, may hold values from -0.5 to 0.5
Outputs:
- attended: bfloat16 [4096, 2048], P(('dp', 'col'), 'row'), parts along dimension 0
There are 4 independent parts, one for each index of `dp`. A program takes and returns all parts, laid end to end along the dimension named above; each array names one. Nothing has to cross between parts.
All inputs are finite; a program needn't handle non-finite values.
Results may differ from a plain program's by a relative error of at most 0.03.
Values may be sent and summed in bfloat16 or wider, within the bound.
A program may use at most 64 MiB of HBM per device.

v0:
```python
import jax
import jax.numpy as jnp
from jax import lax
from jax.sharding import PartitionSpec as P

HEAD_DIM = 128
D = 2048


def per_device(latents, norm_gain, q_weight, k_weight, v_weight, out_weight):
    wide = latents.astype(jnp.float32)
    squares = jnp.sum(wide * wide, axis=1)
    total = lax.psum(squares, "row")
    normed = (wide * lax.rsqrt(total / D + 1e-06)[:, None] * norm_gain[None, :]).astype(
        jnp.bfloat16
    )
    gathered = lax.all_gather(normed, "col", axis=0, tiled=True)
    row_count = lax.axis_size("row")
    columns = q_weight.shape[1]
    inv_root = 1.0 / jnp.sqrt(jnp.float32(HEAD_DIM))

    def attend(query):
        heads_here = query.shape[1] // HEAD_DIM
        query3 = query.reshape(query.shape[0], heads_here, HEAD_DIM)
        initial = (
            jnp.full((heads_here, query.shape[0]), -1e30, jnp.float32),
            jnp.zeros((heads_here, query.shape[0]), jnp.float32),
            jnp.zeros((heads_here, query.shape[0], HEAD_DIM), jnp.float32),
        )

        def update(carry, pieces, start):
            peak, denom, acc = carry
            keys_part, values_part = pieces
            keys3 = keys_part.reshape(keys_part.shape[0], heads_here, HEAD_DIM)
            values3 = values_part.reshape(values_part.shape[0], heads_here, HEAD_DIM)
            scores = (
                jnp.einsum("qhd,khd->hqk", query3, keys3, preferred_element_type=jnp.float32)
                * inv_root
            )
            fresh = jnp.maximum(peak, jnp.max(scores, axis=2))
            weights = jnp.exp(scores - fresh[:, :, None])
            denom = jnp.sum(weights, axis=2)
            acc = jnp.einsum(
                "hqk,khd->hqd",
                weights.astype(jnp.bfloat16),
                values3,
                preferred_element_type=jnp.float32,
            )
            return (fresh, denom, acc)

        return (initial, update)

    quarter = columns // row_count
    width_rows = q_weight.shape[0]
    joined = jnp.stack(
        [
            q_weight.reshape(width_rows, row_count, quarter),
            k_weight.reshape(width_rows, row_count, quarter),
            v_weight.reshape(width_rows, row_count, quarter),
        ],
        axis=2,
    ).reshape(width_rows, 3 * columns)
    partial_value = jnp.dot(gathered, joined, preferred_element_type=jnp.float32).astype(
        jnp.bfloat16
    )
    reduced = (
        lax.psum_scatter(partial_value, "row", scatter_dimension=1, tiled=True)
        .astype(jnp.float32)
        .astype(jnp.bfloat16)
    )
    query = reduced[:, :quarter]
    initial, update = attend(query)
    peak, denom, acc = update(
        initial, (reduced[:, quarter : 2 * quarter], reduced[:, 2 * quarter :]), 0
    )
    mixed = acc / denom[:, :, None]
    mixed = jnp.transpose(mixed, (1, 0, 2)).reshape(query.shape[0], quarter).astype(jnp.bfloat16)
    terms = jnp.dot(
        lax.all_gather(mixed, "row", axis=1, tiled=True),
        out_weight,
        preferred_element_type=jnp.float32,
    ).astype(jnp.bfloat16)
    return (
        lax.psum_scatter(terms, "col", scatter_dimension=0, tiled=True)
        .astype(jnp.float32)
        .astype(jnp.bfloat16)
    )


def solution(mesh):
    return jax.shard_map(
        per_device,
        mesh=mesh,
        in_specs=(
            P(("dp", "col"), "row"),
            P(("dp", "row")),
            P(("dp", "row"), "col"),
            P(("dp", "row"), "col"),
            P(("dp", "row"), "col"),
            P(("dp", "col"), "row"),
        ),
        out_specs=P(("dp", "col"), "row"),
        check_vma=False,
    )
```

profile of v0, /device:TPU:0, one launch (start us, length us, event | category | flops | bytes accessed | tf_op | source)
XLA Modules:
  0.0 167.0 jit_solution(1679290973142191525)
XLA Ops:
  6.5 0.0 copy-start
  6.5 0.0 all-gather.3.cloned.1.call-start
  6.5 1.3 fusion.9
  7.8 8.4 %psum.7 = f32[512]{0:T(512)S(1)} all-reduce(f32[512]{0:T(512)S(1)} %fusion.9), channel_id=1, replica_groups=mesh['dp'=4,'row'=4,'col'=2] {'row'}, use_global_device_ids=true, to_apply=%region_1.0 | all-reduce | flops 512 | bytes 4096 | tf_op jit(solution)/shard_map/psum | solution.py:13
  16.3 2.0 %fusion.11 = bf16[512,512]{1,0:T(8,128)(2,1)} fusion(bf16[512,512]{1,0:T(8,128)(2,1)} %param.6, f32[512]{0:T(512)} %param.7, f32[512]{0:T(512)S(1)} %add_rsqrt_fusion), kind=kLoop, calls=%fused_computation.15 | loop fusion | flops 1048576 | bytes 1052672 | tf_op jit(solution)/shard_map/convert_element_type | solution.py:14
  18.3 0.0 all-gather.3.cloned.1.call-update
  18.3 0.0 reduce-scatter.3.cloned.1.call-start
  18.4 1.5 copy.11
  19.9 1.5 copy.12
  21.4 2.3 %copy.13 = bf16[512,1024]{0,1:T(8,128)(2,1)} copy(bf16[512,1024]{1,0:T(8,128)(2,1)} %param.10) | data formatting | bytes 2097152 | tf_op args[4]
  23.7 3.3 %pad_maximum_fusion = bf16[512,4,3,256]{0,3,2,1:T(8,128)(2,1)} fusion(bf16[512,4,1,256]{0,3,2,1:T(8,128)(2,1)} %bitcast.32, bf16[512,4,1,256]{0,3,2,1:T(8,128)(2,1)S(1)} %bitcast.31, bf16[512,4,1,256]{0,3,2,1:T(8,128)(2,1)S(1)} %bitcast.30), kind=kLoop, calls=%fused_computation.8 | loop fusion | flops 3145728 | bytes 6291456 | tf_op jit(solution)/shard_map/stack | solution.py:55
  27.0 13.0 %all-gather.3.cloned.1.call-done = bf16[1024,512]{1,0:T(8,128)(2,1)} async-done(((bf16[512,512]{1,0:T(8,128)(2,1)}), bf16[1024,512]{1,0:T(8,128)(2,1)}) %all-gather.3.cloned.1.call-update) | async-done | bytes 1048592 | tf_op jit(solution)/shard_map/all_gather | solution.py:17
  40.0 8.3 %convolution_convert_fusion = bf16[1024,3072]{1,0:T(8,128)(2,1)} fusion(bf16[1024,512]{1,0:T(8,128)(2,1)} %all-gather.3.cloned.1.call-done, bf16[512,3072]{0,1:T(8,128)(2,1)} %bitcast.33), kind=kOutput, calls=%fused_computation.4 | convolution fusion | flops 3224371200 | bytes 10485760 | tf_op jit(solution)/shard_map/dot_general | solution.py:63
  48.4 0.0 reduce-scatter.3.cloned.1.call-update
  48.4 0.0 all-gather.5.cloned.1.call-start
  48.4 58.0 %reduce-scatter.3.cloned.1.call-done = bf16[1024,768]{1,0:T(8,128)(2,1)} async-done(((bf16[1024,3072]{1,0:T(8,128)(2,1)}), bf16[1024,768]{1,0:T(8,128)(2,1)}) %reduce-scatter.3.cloned.1.call-update) | async-done | bytes 1572880 | tf_op jit(solution)/shard_map/reduce_scatter | solution.py:67
  106.4 1.6 slice_bitcast_fusion.1
  108.0 0.2 copy.19
  108.2 1.3 multiply_reduce_fusion
  109.5 1.4 fusion
  110.9 2.5 %divide_convert_fusion = bf16[1024,2,128]{0,2,1:T(8,128)(2,1)} fusion(bf16[1024,2,128]{0,2,1:T(8,128)(2,1)S(1)} %bitcast.35, f32[2,1024,1024]{1,2,0:T(8,128)S(1)} %get-tuple-element.9, f32[2,1024]{1,0:T(2,128)S(1)} %broadcast_maximum_fusion, f32[1024,2]{0,1:T(2,128)S(1)} %bitcast.36), kind=kOutput, calls=%fused_computation.16 | convolution fusion | flops 543686656 | bytes 9453568 | tf_op jit(solution)/shard_map/hqk,khd->hqd/dot_general | solution.py:43
  113.4 0.0 all-gather.5.cloned.1.call-update
  113.4 0.0 reduce-scatter.5.cloned.1.call-start
  113.4 22.7 %all-gather.5.cloned.1.call-done = bf16[1024,1024]{0,1:T(8,128)(2,1)} async-done(((bf16[1024,256]{0,1:T(8,128)(2,1)}), bf16[1024,1024]{0,1:T(8,128)(2,1)}) %all-gather.5.cloned.1.call-update) | async-done | bytes 2097168 | tf_op jit(solution)/shard_map/all_gather | solution.py:79
  136.1 0.0 copy-done
  136.1 3.9 %convolution_convert_fusion.1 = bf16[1024,512]{1,0:T(8,128)(2,1)} fusion(bf16[1024,1024]{0,1:T(8,128)(2,1)} %all-gather.5.cloned.1.call-done, bf16[1024,512]{1,0:T(8,128)(2,1)S(1)} %copy-done), kind=kOutput, calls=%fused_computation.9 | convolution fusion | flops 1074266112 | bytes 4194304 | tf_op jit(solution)/shard_map/dot_general | solution.py:78
  139.9 0.0 reduce-scatter.5.cloned.1.call-update
  140.0 20.5 %reduce-scatter.5.cloned.1.call-done = bf16[512,512]{1,0:T(8,128)(2,1)} async-done(((bf16[1024,512]{1,0:T(8,128)(2,1)}), bf16[512,512]{1,0:T(8,128)(2,1)}) %reduce-scatter.5.cloned.1.call-update) | async-done | bytes 524304 | tf_op jit(solution)/shard_map/reduce_scatter | solution.py:84
  (2 shorter events, 0.0 us)
Async XLA Ops:
  6.5 129.5 %copy-start = (bf16[1024,512]{1,0:T(8,128)(2,1)S(1)}, bf16[1024,512]{1,0:T(8,128)(2,1)}, u32[]{:S(2)}) copy-start(bf16[1024,512]{1,0:T(8,128)(2,1)} %param.11) | copy-start | bytes 3145732
  6.5 33.5 %all-gather.3.cloned.1.call-start = ((), (), s32[]{:S(2)}) async-start(), calls=%async_computation.2 | async-start | bytes 1572864 | tf_op jit(solution)/shard_map/all_gather | solution.py:17
  18.3 88.1 %reduce-scatter.3.cloned.1.call-start = ((), (), s32[]{:S(2)}) async-start(), calls=%async_computation.3 | async-start | bytes 7864320 | tf_op jit(solution)/shard_map/reduce_scatter | solution.py:67
  48.4 87.7 %all-gather.5.cloned.1.call-start = ((), (), s32[]{:S(2)}) async-start(), calls=%async_computation.4 | async-start | bytes 2621440 | tf_op jit(solution)/shard_map/all_gather | solution.py:79
  113.4 47.1 %reduce-scatter.5.cloned.1.call-start = ((), (), s32[]{:S(2)}) async-start(), calls=%async_computation.5 | async-start | bytes 1572864 | tf_op jit(solution)/shard_map/reduce_scatter | solution.py:84
Sparse Core Ops, SparseCore 0:
  18.4 21.5 all-gather.2
  48.5 57.8 reduce-scatter.2
  113.5 22.5 all-gather.4
  140.1 20.3 reduce-scatter.4
where the time goes:
time: 167 us
  waiting for transfers between devices  114 us (68%)
  matrix products  15.9 us (10%)
  between operations  13.2 us (8%)
  blocking collectives  8.4 us (5%)
  other arithmetic  8.05 us (5%)
  local copies, waits for them, and re-layouts  7.08 us (4%)
    reduce_scatter x1, waiting for transfers between devices, per_device(): lax.psum_scatter(partial_value, 'row', scatter_dimension=1, tiled=True)  58 us
    all_gather x1, waiting for transfers between devices, per_device(): lax.all_gather(mixed, 'row', axis=1, tiled=True)  22.7 us
    reduce_scatter x1, waiting for transfers between devices, per_device(): lax.psum_scatter(terms, 'col', scatter_dimension=0, tiled=True)  20.5 us
    all_gather x1, waiting for transfers between devices, per_device(): gathered = lax.all_gather(normed, 'col', axis=0, tiled=True)  13 us
    psum x1, blocking collectives, per_device(): total = lax.psum(squares, 'row')  8.4 us
    dot_general x1, matrix products, per_device(): jnp.dot(gathered, joined, preferred_element_type=jnp.float32)  8.33 us
    unnamed x6, local copies, waits for them, and re-layouts  6.87 us
    dot_general x1, matrix products, per_device(): jnp.dot(lax.all_gather(mixed, 'row', axis=1, tiled=True), out_weight, pre...  3.86 us
  transfers between devices with their start and end apart: 4, of which 4 were waited for; matrix products, arithmetic and copies ran while one was open for 5% of the time, Pallas kernels for 0%

commit v1 on v0

v1 whole, which is shorter than its diff:
```python
import functools
import math

import jax
import jax.numpy as jnp
from jax import lax
from jax.experimental import pallas as pl
from jax.experimental.pallas import tpu as pltpu
from jax.sharding import PartitionSpec as P

HEAD_DIM = 128
EPS = 1e-06
MESH = pl.DeviceIdType.MESH
F32 = jnp.float32
BF16 = jnp.bfloat16
KEY, VALUE, QUERY = 0, 1, 2


def kernel(
    row_count, chunk,
    x_hbm, gain_hbm, k_hbm, v_hbm, q_hbm, o_hbm, out_ref,
    xraw, gains, wbuf, wo, xg, ssq, ssq_out, ssq_in, scale, psend, precv, pown,
    qkv, mix, osend, orecv,
    l_sem, x_send, x_recv, w_send, w_recv, s_send, s_recv, p_send, p_recv,
    my_send, my_recv, mc_send, mc_recv, mf_send, mf_recv, o_send, o_recv,
):
    rows, width = x_hbm.shape
    quarter = wbuf.shape[3]
    heads_here = quarter // HEAD_DIM
    features = width * row_count
    per_half = rows // chunk

    row = lax.axis_index("row")
    col = lax.axis_index("col")
    y, c = row // 2, row % 2
    pair = {"row": 2 * y + (1 - c)}
    ypeer = {"row": 2 * (1 - y) + c}
    xpeer = {"col": 1 - col}

    def span(y_of, c_of):
        return pl.ds(pl.multiple_of((2 * y_of + c_of) * quarter, quarter), quarter)

    def remote(src, dst, send, recv, device):
        return pltpu.make_async_remote_copy(
            src_ref=src, dst_ref=dst, send_sem=send, recv_sem=recv,
            device_id=device, device_id_type=MESH)

    weights = (k_hbm, v_hbm, q_hbm)
    y_of = (1 - y, y)

    local = [
        pltpu.make_async_copy(x_hbm, xraw.at[0, 0], l_sem.at[0]),
        pltpu.make_async_copy(gain_hbm, gains.at[0], l_sem.at[1]),
    ]
    w_local = {}
    for side in range(2):
        for t in range(3):
            w_local[side, t] = pltpu.make_async_copy(
                weights[t].at[:, span(y_of[side], c)],
                wbuf.at[side, t, pl.ds(0, width)], l_sem.at[3 + side * 3 + t])
    wo_local = pltpu.make_async_copy(o_hbm, wo, l_sem.at[2])
    for copy in local:
        copy.start()
    for copy in w_local.values():
        copy.start()
    wo_local.start()

    barrier = pltpu.get_barrier_semaphore()
    for device in (pair, ypeer, xpeer):
        pl.semaphore_signal(barrier, inc=1, device_id=device, device_id_type=MESH)
    pl.semaphore_wait(barrier, 3)

    x_to_x = remote(x_hbm, xraw.at[1, 0], x_send.at[0], x_recv.at[0], xpeer)
    x_to_pair = remote(x_hbm, xraw.at[0, 1], x_send.at[1], x_recv.at[1], pair)
    g_to_pair = remote(gain_hbm, gains.at[1], x_send.at[2], x_recv.at[2], pair)
    x_forward = remote(xraw.at[1, 0], xraw.at[1, 1], x_send.at[3], x_recv.at[3], pair)
    w_pair = {}
    for side in range(2):
        for t in range(3):
            w_pair[side, t] = remote(
                weights[t].at[:, span(y_of[side], 1 - c)],
                wbuf.at[side, t, pl.ds(width, width)],
                w_send.at[side * 3 + t], w_recv.at[side * 3 + t], pair)
    x_to_x.start()
    g_to_pair.start()
    x_to_pair.start()
    for side in range(2):
        for t in range(3):
            w_pair[side, t].start()

    def prepare(half, part):
        gain = gains[part]

        @pl.loop(0, per_half)
        def _(j):
            at = pl.ds(pl.multiple_of(j * chunk, chunk), chunk)
            wide = xraw[half, part, at, :].astype(F32)
            total = jnp.broadcast_to(
                jnp.sum(wide * wide, axis=1, keepdims=True), (chunk, 128))
            if part == 0:
                ssq[half, at, :] = total
            else:
                ssq[half, at, :] += total
            xg[half, at, pl.ds(part * width, width)] = (wide * gain).astype(BF16)

    def squares(half):
        return remote(ssq_out.at[half], ssq_in.at[half], s_send.at[half], s_recv.at[half], ypeer)

    def send_squares(half):
        ssq_out[half] = jnp.transpose(ssq[half])[0:8, :]
        squares(half).start()

    def partial(half, t):
        return remote(psend.at[half, t], precv.at[half, t],
                      p_send.at[half, t], p_recv.at[half, t], ypeer)

    def product(half, side, t):
        return jnp.dot(xg[half], wbuf[side, t], preferred_element_type=F32)

    def away(half, t):
        psend[half, t] = product(half, 0, t).astype(BF16)
        partial(half, t).start()

    def home(half, t):
        pown[half, t] = product(half, 1, t)

    for copy in local:
        copy.wait()
    prepare(0, 0)
    g_to_pair.wait_recv()
    x_to_pair.wait_recv()
    prepare(0, 1)
    for t in range(2):
        w_local[0, t].wait()
        w_pair[0, t].wait_recv()
        away(0, t)
    send_squares(0)
    for t in range(3):
        w_local[1, t].wait()
        w_pair[1, t].wait_recv()
    w_local[0, QUERY].wait()
    w_pair[0, QUERY].wait_recv()

    @pl.loop(0, 3)
    def _(t):
        home(0, t)

    x_to_x.wait_recv()
    x_forward.start()
    prepare(1, 0)
    x_forward.wait_recv()
    prepare(1, 1)

    @pl.loop(0, 3)
    def _(t):
        away(1, t)

    away(0, QUERY)
    send_squares(1)

    @pl.loop(0, 3)
    def _(t):
        home(1, t)

    for half in range(2):
        squares(half).wait_recv()
        arrived = jnp.transpose(jnp.broadcast_to(ssq_in[half, 0:1, :], (128, rows)))
        scale[half] = lax.rsqrt((ssq[half] + arrived) / features + EPS)

    to_exponent = math.log2(math.e) / math.sqrt(HEAD_DIM)

    def combine(half, t):
        partial(half, t).wait_recv()
        factor = scale[half]
        if t == QUERY:
            factor = factor * to_exponent
        for h in range(heads_here):
            lanes = pl.ds(h * HEAD_DIM, HEAD_DIM)
            added = pown[half, t, :, lanes] + precv[half, t, :, lanes].astype(F32)
            qkv[t, pl.ds(half * rows, rows), lanes] = (added * factor).astype(BF16)

    def mixed(half, j, y_at, c_at):
        return mix.at[half, pl.ds(pl.multiple_of(j * chunk, chunk), chunk), span(y_at, c_at)]

    def mixed_y(half, j):
        block = mixed(half, j, y, c)
        return remote(block, block, my_send.at[half, j], my_recv.at[half, j], ypeer)

    def mixed_pair(half, j):
        block = mixed(half, j, y, c)
        return remote(block, block, mc_send.at[half, j], mc_recv.at[half, j], pair)

    def mixed_forward(half, j):
        block = mixed(half, j, 1 - y, c)
        return remote(block, block, mf_send.at[half, j], mf_recv.at[half, j], pair)

    def attend(half):
        @pl.loop(0, per_half)
        def _(j):
            at = pl.ds(pl.multiple_of(half * rows + j * chunk, chunk), chunk)
            parts = []
            for h in range(heads_here):
                lanes = pl.ds(h * HEAD_DIM, HEAD_DIM)
                scores = lax.dot_general(
                    qkv[QUERY, at, lanes], qkv[KEY, :, lanes],
                    (((1,), (1,)), ((), ())), preferred_element_type=F32)
                peak = jnp.max(scores, axis=1, keepdims=True)
                weight = jnp.exp2(scores - peak)
                denom = jnp.sum(weight, axis=1, keepdims=True)
                acc = jnp.dot(weight.astype(BF16), qkv[VALUE, :, lanes],
                              preferred_element_type=F32)
                parts.append((acc / denom).astype(BF16))
            mix[half, pl.ds(pl.multiple_of(j * chunk, chunk), chunk), span(y, c)] = (
                jnp.concatenate(parts, axis=1))
            mixed_y(half, j).start()
            mixed_pair(half, j).start()

    for half in range(2):
        for t in (KEY, VALUE):
            combine(half, t)
    for half in (1, 0):
        combine(half, QUERY)
        attend(half)

    wo_local.wait()

    def out_copy(j):
        return remote(osend.at[j], orecv.at[j], o_send.at[j], o_recv.at[j], xpeer)

    for half in (1, 0):
        @pl.loop(0, per_half)
        def _(j):
            mixed_y(half, j).wait_recv()
            mixed_forward(half, j).start()

        @pl.loop(0, per_half)
        def _(j):
            mixed_pair(half, j).wait_recv()
            mixed_forward(half, j).wait_recv()
            at = pl.ds(pl.multiple_of(j * chunk, chunk), chunk)
            terms = jnp.dot(mix[half, at, :], wo[...], preferred_element_type=F32)
            if half == 1:
                osend[j] = terms.astype(BF16)
                out_copy(j).start()
            else:
                out_copy(j).wait_recv()
                out_ref[at, :] = (terms + orecv[j].astype(F32)).astype(BF16)

    for copy in (x_to_x, x_to_pair, g_to_pair, x_forward):
        copy.wait_send()
    for copy in w_pair.values():
        copy.wait_send()
    for half in range(2):
        squares(half).wait_send()
        for t in range(3):
            partial(half, t).wait_send()
        for j in range(per_half):
            mixed_y(half, j).wait_send()
            mixed_pair(half, j).wait_send()
            mixed_forward(half, j).wait_send()
    for j in range(per_half):
        out_copy(j).wait_send()


def per_device(latents, norm_gain, q_weight, k_weight, v_weight, out_weight):
    row_count = lax.axis_size("row")
    assert row_count == 4 and lax.axis_size("col") == 2
    rows, width = latents.shape
    quarter = q_weight.shape[1] // row_count
    held = out_weight.shape[0]
    out_width = out_weight.shape[1]
    chunk = rows // 2
    per_half = rows // chunk
    dma = pltpu.SemaphoreType.DMA
    vmem = pltpu.VMEM
    scratch = [
        vmem((2, 2, rows, width), BF16),
        vmem((2, 1, width), F32),
        vmem((2, 3, 2 * width, quarter), BF16),
        vmem((held, out_width), BF16),
        vmem((2, rows, 2 * width), BF16),
        vmem((2, rows, 128), F32),
        vmem((2, 8, rows), F32),
        vmem((2, 8, rows), F32),
        vmem((2, rows, 128), F32),
        vmem((2, 3, rows, quarter), BF16),
        vmem((2, 3, rows, quarter), BF16),
        vmem((2, 3, rows, quarter), F32),
        vmem((3, 2 * rows, quarter), BF16),
        vmem((2, rows, held), BF16),
        vmem((per_half, chunk, out_width), BF16),
        vmem((per_half, chunk, out_width), BF16),
        dma((9,)),
        dma((4,)), dma((4,)),
        dma((6,)), dma((6,)),
        dma((2,)), dma((2,)),
        dma((2, 3)), dma((2, 3)),
    ] + [dma((2, per_half))] * 6 + [dma((per_half,))] * 2
    return pl.pallas_call(
        functools.partial(kernel, row_count, chunk),
        out_shape=jax.ShapeDtypeStruct((rows, out_width), BF16),
        in_specs=[pl.BlockSpec(memory_space=pl.ANY)] * 6,
        out_specs=pl.BlockSpec(memory_space=pltpu.VMEM),
        scratch_shapes=scratch,
        compiler_params=pltpu.CompilerParams(
            collective_id=0, has_side_effects=True, vmem_limit_bytes=60 * 1024 * 1024),
    )(latents, norm_gain.reshape(1, width), k_weight, v_weight, q_weight, out_weight)


def solution(mesh):
    return jax.shard_map(
        per_device,
        mesh=mesh,
        in_specs=(
            P(("dp", "col"), "row"),
            P(("dp", "row")),
            P(("dp", "row"), "col"),
            P(("dp", "row"), "col"),
            P(("dp", "row"), "col"),
            P(("dp", "col"), "row"),
        ),
        out_specs=P(("dp", "col"), "row"),
        check_vma=False,
    )
```

time: 167 us -> 68.8 us (0.41)
  waiting for transfers between devices: 114 us -> 0 us
  Pallas kernels: 0 us -> 66.8 us
  matrix products: 15.9 us -> 0 us
  between operations: 13.2 us -> 0.01 us
  blocking collectives: 8.4 us -> 0 us
  other arithmetic: 8.05 us -> 0 us
  local copies, waits for them, and re-layouts: 7.08 us -> 1.87 us
    reduce_scatter x2 -> x0, waiting for transfers between devices: 78.5 us -> none  [the longest x1 58 us: per_device(): lax.psum_scatter(partial_value, 'row', scatter_dimension=1, tiled=True)]
    pallas_call x0 -> x1, Pallas kernels: none -> 66.8 us  [per_device(): pl.pallas_call(functools.partial(kernel, row_count, chunk), out_shape=jax...]
    all_gather x2 -> x0, waiting for transfers between devices: 35.7 us -> none  [the longest x1 22.7 us: per_device(): lax.all_gather(mixed, 'row', axis=1, tiled=True)]
    dot_general x4 -> x0, matrix products: 15.9 us -> none  [the longest x1 8.33 us: per_device(): jnp.dot(gathered, joined, preferred_element_type=jnp.float32)]
    psum x1 -> x0, blocking collectives: 8.4 us -> none  [per_device(): total = lax.psum(squares, 'row')]
    unnamed x6 -> x1, local copies, waits for them, and re-layouts: 6.87 us -> 1.87 us
    another operation x2 -> x0, other arithmetic: 3.33 us -> none  [the longest x1 3.32 us: per_device(): jnp.stack([q_weight.reshape(width_rows, row_count, quarter), k_weight.res...]
    reduce_sum x2 -> x0, other arithmetic: 2.69 us -> none  [the longest x1 1.38 us: update(): denom = jnp.sum(weights, axis=2)]
  transfers between devices with their start and end apart: 4 -> 0, of which waited for: 4 -> 0; matrix products, arithmetic and copies ran while one was open for 5% -> 0% of each run, Pallas kernels for 0% -> 0%
where the time goes in v1:
time: 68.8 us; the launch traced here: 68.7 us
  Pallas kernels  66.8 us (97%)
  local copies, waits for them, and re-layouts  1.87 us (3%)
    pallas_call x1, Pallas kernels, per_device(): pl.pallas_call(functools.partial(kernel, row_count, chunk), out_shape=jax...  66.8 us
    unnamed x1, local copies, waits for them, and re-layouts  1.87 us

profile of v1, /device:TPU:0, one launch (start us, length us, event | category | flops | bytes accessed | tf_op | source)
XLA Modules:
  0.0 68.7 jit_solution(9520139519398812711)
XLA Ops:
  0.0 66.8 %shard_map.64 = bf16[512,512]{1,0:T(8,128)(2,1)} custom-call(bf16[512,512]{1,0:T(8,128)(2,1)} %x_hbm.1, f32[1,512]{1,0:T(1,128)} %bitcast.1, bf16[512,1024]{1,0:T(8,128)(2,1)} %k_hbm.1, bf16[512,1024]{1,0:T(8,128)(2,1)} %v_hbm.1, bf16[512,1024]{1,0:T(8,128)(2,1)} %q_hbm.1, bf16[1024,512]{1,0:T(8,128)(2,1)} %o_hbm.1), custom_call_target="tpu_custom_call" | custom-call | tf_op jit(solution)/shard_map/pallas_call | solution.py:299
  66.8 1.9 %copy.8 = bf16[512,512]{1,0:T(8,128)(2,1)} copy(bf16[512,512]{1,0:T(8,128)(2,1)} %shard_map.64) | data formatting | bytes 1048576

commit v2 on v1

v2 whole, which is shorter than its diff:
```python
import functools
import math

import jax
import jax.numpy as jnp
from jax import lax
from jax.experimental import pallas as pl
from jax.experimental.pallas import tpu as pltpu
from jax.sharding import PartitionSpec as P

HEAD_DIM = 128
EPS = 1e-06
MESH = pl.DeviceIdType.MESH
F32 = jnp.float32
BF16 = jnp.bfloat16
KEY, VALUE, QUERY = 0, 1, 2


def kernel(
    row_count, chunk,
    x_hbm, gain_hbm, k_hbm, v_hbm, q_hbm, o_hbm, out_ref,
    xraw, gains, wbuf, wo, xg, ssq, ssq_out, ssq_in, scale, psend, precv, pown,
    qkv, mix, osend, orecv, oown,
    l_sem, g_send, g_recv, x_send, x_recv, w_send, w_recv, s_send, s_recv,
    p_send, p_recv, m_send, m_recv, o_send, o_recv,
):
    rows, width = x_hbm.shape
    quarter = wbuf.shape[3]
    heads_here = quarter // HEAD_DIM
    features = width * row_count
    per_half = rows // chunk

    row = lax.axis_index("row")
    col = lax.axis_index("col")
    y, c = row // 2, row % 2
    pair = {"row": 2 * y + (1 - c)}
    ypeer = {"row": 2 * (1 - y) + c}
    xpeer = {"col": 1 - col}

    def span(y_of, c_of):
        return pl.ds(pl.multiple_of((2 * y_of + c_of) * quarter, quarter), quarter)

    def remote(src, dst, send, recv, device):
        return pltpu.make_async_remote_copy(
            src_ref=src, dst_ref=dst, send_sem=send, recv_sem=recv,
            device_id=device, device_id_type=MESH)

    weights = (k_hbm, v_hbm, q_hbm)
    y_of = (1 - y, y)

    def rows_of(g):
        return pl.ds(pl.multiple_of(g * chunk, chunk), chunk)

    x_local = [
        pltpu.make_async_copy(x_hbm.at[rows_of(g)], xraw.at[g, 0], l_sem.at[8 + g])
        for g in range(per_half)
    ]
    g_local = pltpu.make_async_copy(gain_hbm, gains.at[0], l_sem.at[0])
    w_local = {}
    for side in range(2):
        for t in range(3):
            w_local[side, t] = pltpu.make_async_copy(
                weights[t].at[:, span(y_of[side], c)],
                wbuf.at[side, t, pl.ds(0, width)], l_sem.at[2 + side * 3 + t])
    wo_local = pltpu.make_async_copy(o_hbm, wo, l_sem.at[1])
    g_local.start()
    for copy in x_local:
        copy.start()
    for copy in w_local.values():
        copy.start()
    wo_local.start()

    barrier = pltpu.get_barrier_semaphore()
    for device in (pair, ypeer, xpeer):
        pl.semaphore_signal(barrier, inc=1, device_id=device, device_id_type=MESH)
    pl.semaphore_wait(barrier, 3)

    g_to_pair = remote(gain_hbm, gains.at[1], g_send.at[0], g_recv.at[0], pair)
    x_to_x, x_to_pair, x_forward = [], [], []
    for g in range(per_half):
        x_to_pair.append(remote(
            x_hbm.at[rows_of(g)], xraw.at[g, 1], x_send.at[0, g], x_recv.at[0, g], pair))
        x_to_x.append(remote(
            x_hbm.at[rows_of(g)], xraw.at[per_half + g, 0],
            x_send.at[1, g], x_recv.at[1, g], xpeer))
        x_forward.append(remote(
            xraw.at[per_half + g, 0], xraw.at[per_half + g, 1],
            x_send.at[2, g], x_recv.at[2, g], pair))
    w_pair = {}
    for side in range(2):
        for t in range(3):
            w_pair[side, t] = remote(
                weights[t].at[:, span(y_of[side], 1 - c)],
                wbuf.at[side, t, pl.ds(width, width)],
                w_send.at[side * 3 + t], w_recv.at[side * 3 + t], pair)
    g_to_pair.start()
    for copy in x_to_pair:
        copy.start()
    for copy in x_to_x:
        copy.start()
    for side in range(2):
        for t in range(3):
            w_pair[side, t].start()

    def prepare(g, part):
        wide = xraw[g, part].astype(F32)
        total = jnp.broadcast_to(jnp.sum(wide * wide, axis=1, keepdims=True), (chunk, 128))
        if part == 0:
            ssq[g] = total
        else:
            ssq[g] += total
        xg[g, :, pl.ds(part * width, width)] = (wide * gains[part]).astype(BF16)

    def squares(g):
        return remote(ssq_out.at[g], ssq_in.at[g], s_send.at[g], s_recv.at[g], ypeer)

    def send_squares(g):
        ssq_out[g] = jnp.transpose(ssq[g])[0:8, :]
        squares(g).start()

    def partial(g, t):
        return remote(psend.at[g, t], precv.at[g, t], p_send.at[g, t], p_recv.at[g, t], ypeer)

    def product(g, side, t):
        return jnp.dot(xg[g], wbuf[side, t], preferred_element_type=F32)

    def away(g, t):
        psend[g, t] = product(g, 0, t).astype(BF16)
        partial(g, t).start()

    def home(first):
        @pl.loop(0, per_half)
        def _(g):
            @pl.loop(0, 3)
            def _(t):
                pown[first + g, t] = product(first + g, 1, t)

    near = range(per_half)
    far = range(per_half, 2 * per_half)

    g_local.wait()
    for g in near:
        x_local[g].wait()
        prepare(g, 0)
        if g == 0:
            g_to_pair.wait_recv()
        x_to_pair[g].wait_recv()
        prepare(g, 1)
        if g == 0:
            w_local[0, KEY].wait()
            w_pair[0, KEY].wait_recv()
        away(g, KEY)
    w_local[0, VALUE].wait()
    w_pair[0, VALUE].wait_recv()
    for g in near:
        away(g, VALUE)
        send_squares(g)
    for t in range(3):
        w_local[1, t].wait()
        w_pair[1, t].wait_recv()
    home(0)
    w_local[0, QUERY].wait()
    w_pair[0, QUERY].wait_recv()

    for g in far:
        x_to_x[g - per_half].wait_recv()
        x_forward[g - per_half].start()
        prepare(g, 0)
        x_forward[g - per_half].wait_recv()
        prepare(g, 1)
        for t in (KEY, VALUE):
            away(g, t)
        send_squares(g)
    for g in far:
        away(g, QUERY)
    away(0, QUERY)
    home(per_half)

    to_exponent = math.log2(math.e) / math.sqrt(HEAD_DIM)

    def combine(g, t):
        partial(g, t).wait_recv()
        factor = scale[g]
        if t == QUERY:
            factor = factor * to_exponent
        for h in range(heads_here):
            lanes = pl.ds(h * HEAD_DIM, HEAD_DIM)
            added = pown[g, t, :, lanes] + precv[g, t, :, lanes].astype(F32)
            qkv[t, rows_of(g), lanes] = (added * factor).astype(BF16)

    for g in (*near, *far):
        squares(g).wait_recv()
        arrived = jnp.transpose(jnp.broadcast_to(ssq_in[g, 0:1, :], (128, chunk)))
        scale[g] = lax.rsqrt((ssq[g] + arrived) / features + EPS)
        for t in (KEY, VALUE):
            combine(g, t)

    def mixed_y(g):
        block = mix.at[g, :, span(y, c)]
        return remote(block, block, m_send.at[0, g], m_recv.at[0, g], ypeer)

    def mixed_pair(g):
        block = mix.at[g, :, span(y, c)]
        return remote(block, block, m_send.at[1, g], m_recv.at[1, g], pair)

    def mixed_forward(g):
        block = mix.at[g, :, span(1 - y, c)]
        return remote(block, block, m_send.at[2, g], m_recv.at[2, g], pair)

    def attend(g):
        combine(g, QUERY)
        parts = []
        for h in range(heads_here):
            lanes = pl.ds(h * HEAD_DIM, HEAD_DIM)
            scores = lax.dot_general(
                qkv[QUERY, rows_of(g), lanes], qkv[KEY, :, lanes],
                (((1,), (1,)), ((), ())), preferred_element_type=F32)
            peak = jnp.max(scores, axis=1, keepdims=True)
            weight = jnp.exp2(scores - peak)
            denom = jnp.sum(weight, axis=1, keepdims=True)
            acc = jnp.dot(weight.astype(BF16), qkv[VALUE, :, lanes],
                          preferred_element_type=F32)
            parts.append((acc / denom).astype(BF16))
        mix[g, :, span(y, c)] = jnp.concatenate(parts, axis=1)
        mixed_y(g).start()
        mixed_pair(g).start()

    def forward(g):
        mixed_y(g).wait_recv()
        mixed_forward(g).start()

    def terms(g):
        mixed_pair(g).wait_recv()
        mixed_forward(g).wait_recv()
        return jnp.dot(mix[g], wo[...], preferred_element_type=F32)

    def out_copy(g):
        return remote(osend.at[g], orecv.at[g], o_send.at[g], o_recv.at[g], xpeer)

    def out_away(g):
        osend[g - per_half] = terms(g).astype(BF16)
        out_copy(g - per_half).start()

    for g in far:
        attend(g)
    for g in near[1:]:
        away(g, QUERY)
    attend(0)
    wo_local.wait()
    for g in far:
        forward(g)
        out_away(g)
    for g in near[1:]:
        attend(g)
    for g in near:
        forward(g)
        oown[g] = terms(g)
    for g in near:
        out_copy(g).wait_recv()
        out_ref[rows_of(g), :] = (oown[g] + orecv[g].astype(F32)).astype(BF16)

    g_to_pair.wait_send()
    for copy in (*x_to_x, *x_to_pair, *x_forward, *w_pair.values()):
        copy.wait_send()
    for g in (*near, *far):
        squares(g).wait_send()
        for t in range(3):
            partial(g, t).wait_send()
        mixed_y(g).wait_send()
        mixed_pair(g).wait_send()
        mixed_forward(g).wait_send()
    for g in near:
        out_copy(g).wait_send()


def per_device(latents, norm_gain, q_weight, k_weight, v_weight, out_weight):
    row_count = lax.axis_size("row")
    assert row_count == 4 and lax.axis_size("col") == 2
    rows, width = latents.shape
    quarter = q_weight.shape[1] // row_count
    held = out_weight.shape[0]
    out_width = out_weight.shape[1]
    chunk = rows // 2
    per_half = rows // chunk
    dma = pltpu.SemaphoreType.DMA
    vmem = pltpu.VMEM
    pieces = 2 * per_half
    scratch = [
        vmem((pieces, 2, chunk, width), BF16),
        vmem((2, 1, width), F32),
        vmem((2, 3, 2 * width, quarter), BF16),
        vmem((held, out_width), BF16),
        vmem((pieces, chunk, 2 * width), BF16),
        vmem((pieces, chunk, 128), F32),
        vmem((pieces, 8, chunk), F32),
        vmem((pieces, 8, chunk), F32),
        vmem((pieces, chunk, 128), F32),
        vmem((pieces, 3, chunk, quarter), BF16),
        vmem((pieces, 3, chunk, quarter), BF16),
        vmem((pieces, 3, chunk, quarter), F32),
        vmem((3, 2 * rows, quarter), BF16),
        vmem((pieces, chunk, held), BF16),
        vmem((per_half, chunk, out_width), BF16),
        vmem((per_half, chunk, out_width), BF16),
        vmem((per_half, chunk, out_width), F32),
        dma((8 + per_half,)),
        dma((1,)), dma((1,)),
        dma((3, per_half)), dma((3, per_half)),
        dma((6,)), dma((6,)),
        dma((pieces,)), dma((pieces,)),
        dma((pieces, 3)), dma((pieces, 3)),
        dma((3, pieces)), dma((3, pieces)),
        dma((per_half,)), dma((per_half,)),
    ]
    return pl.pallas_call(
        functools.partial(kernel, row_count, chunk),
        out_shape=jax.ShapeDtypeStruct((rows, out_width), BF16),
        in_specs=[pl.BlockSpec(memory_space=pl.ANY)] * 6,
        out_specs=pl.BlockSpec(memory_space=pltpu.VMEM),
        scratch_shapes=scratch,
        compiler_params=pltpu.CompilerParams(
            collective_id=0, has_side_effects=True, vmem_limit_bytes=60 * 1024 * 1024),
    )(latents, norm_gain.reshape(1, width), k_weight, v_weight, q_weight, out_weight)


def solution(mesh):
    return jax.shard_map(
        per_device,
        mesh=mesh,
        in_specs=(
            P(("dp", "col"), "row"),
            P(("dp", "row")),
            P(("dp", "row"), "col"),
            P(("dp", "row"), "col"),
            P(("dp", "row"), "col"),
            P(("dp", "col"), "row"),
        ),
        out_specs=P(("dp", "col"), "row"),
        check_vma=False,
    )
```

time: 68.8 us -> 61 us (0.89)
  Pallas kernels: 66.8 us -> 59 us
    pallas_call x1, Pallas kernels: 66.8 us -> 59 us  [per_device(): pl.pallas_call(functools.partial(kernel, row_count, chunk), out_shape=jax...]
where the time goes in v2:
time: 61 us; the launch traced here: 60.9 us
  Pallas kernels  59 us (97%)
  local copies, waits for them, and re-layouts  1.87 us (3%)
    pallas_call x1, Pallas kernels, per_device(): pl.pallas_call(functools.partial(kernel, row_count, chunk), out_shape=jax...  59 us
    unnamed x1, local copies, waits for them, and re-layouts  1.87 us

profile of v2, /device:TPU:0, one launch (start us, length us, event | category | flops | bytes accessed | tf_op | source)
XLA Modules:
  0.0 60.9 jit_solution(13070913485347225943)
XLA Ops:
  0.0 59.0 %shard_map.64 = bf16[512,512]{1,0:T(8,128)(2,1)} custom-call(bf16[512,512]{1,0:T(8,128)(2,1)} %x_hbm.1, f32[1,512]{1,0:T(1,128)} %bitcast.1, bf16[512,1024]{1,0:T(8,128)(2,1)} %k_hbm.1, bf16[512,1024]{1,0:T(8,128)(2,1)} %v_hbm.1, bf16[512,1024]{1,0:T(8,128)(2,1)} %q_hbm.1, bf16[1024,512]{1,0:T(8,128)(2,1)} %o_hbm.1), custom_call_target="tpu_custom_call" | custom-call | tf_op jit(solution)/shard_map/pallas_call | solution.py:315
  59.0 1.9 %copy.8 = bf16[512,512]{1,0:T(8,128)(2,1)} copy(bf16[512,512]{1,0:T(8,128)(2,1)} %shard_map.64) | data formatting | bytes 1048576

commit v3 on v2

--- a/solution.py
+++ b/solution.py
@@ -20,7 +20,7 @@
     row_count, chunk,
     x_hbm, gain_hbm, k_hbm, v_hbm, q_hbm, o_hbm, out_ref,
     xraw, gains, wbuf, wo, xg, ssq, ssq_out, ssq_in, scale, psend, precv, pown,
-    qkv, mix, osend, orecv, oown,
+    qkv, mix, osend, orecv, oown, oout,
     l_sem, g_send, g_recv, x_send, x_recv, w_send, w_recv, s_send, s_recv,
     p_send, p_recv, m_send, m_recv, o_send, o_recv,
 ):
@@ -93,14 +93,13 @@
                 weights[t].at[:, span(y_of[side], 1 - c)],
                 wbuf.at[side, t, pl.ds(width, width)],
                 w_send.at[side * 3 + t], w_recv.at[side * 3 + t], pair)
+    x_to_pair[0].start()
     g_to_pair.start()
-    for copy in x_to_pair:
+    w_pair[0, KEY].start()
+    for copy in (*x_to_x, *x_to_pair[1:]):
         copy.start()
-    for copy in x_to_x:
+    for copy in list(w_pair.values())[1:]:
         copy.start()
-    for side in range(2):
-        for t in range(3):
-            w_pair[side, t].start()
 
     def prepare(g, part):
         wide = xraw[g, part].astype(F32)
@@ -115,7 +114,7 @@
         return remote(ssq_out.at[g], ssq_in.at[g], s_send.at[g], s_recv.at[g], ypeer)
 
     def send_squares(g):
-        ssq_out[g] = jnp.transpose(ssq[g])[0:8, :]
+        ssq_out[g] = jnp.transpose(ssq[g])[0:1, :]
         squares(g).start()
 
     def partial(g, t):
@@ -142,6 +141,7 @@
     for g in near:
         x_local[g].wait()
         prepare(g, 0)
+    for g in near:
         if g == 0:
             g_to_pair.wait_recv()
         x_to_pair[g].wait_recv()
@@ -173,7 +173,6 @@
         send_squares(g)
     for g in far:
         away(g, QUERY)
-    away(0, QUERY)
     home(per_half)
 
     to_exponent = math.log2(math.e) / math.sqrt(HEAD_DIM)
@@ -190,7 +189,7 @@
 
     for g in (*near, *far):
         squares(g).wait_recv()
-        arrived = jnp.transpose(jnp.broadcast_to(ssq_in[g, 0:1, :], (128, chunk)))
+        arrived = jnp.transpose(jnp.broadcast_to(ssq_in[g], (128, chunk)))
         scale[g] = lax.rsqrt((ssq[g] + arrived) / features + EPS)
         for t in (KEY, VALUE):
             combine(g, t)
@@ -225,14 +224,17 @@
         mixed_y(g).start()
         mixed_pair(g).start()
 
-    def forward(g):
+    def chip_terms(g, y_at):
+        held = pl.ds(pl.multiple_of(2 * y_at * quarter, 2 * quarter), 2 * quarter)
+        return jnp.dot(mix[g, :, held], wo[held, :], preferred_element_type=F32)
+
+    def terms(g):
         mixed_y(g).wait_recv()
         mixed_forward(g).start()
-
-    def terms(g):
         mixed_pair(g).wait_recv()
+        oown[g] = chip_terms(g, y)
         mixed_forward(g).wait_recv()
-        return jnp.dot(mix[g], wo[...], preferred_element_type=F32)
+        return oown[g] + chip_terms(g, 1 - y)
 
     def out_copy(g):
         return remote(osend.at[g], orecv.at[g], o_send.at[g], o_recv.at[g], xpeer)
@@ -241,23 +243,25 @@
         osend[g - per_half] = terms(g).astype(BF16)
         out_copy(g - per_half).start()
 
-    for g in far:
-        attend(g)
-    for g in near[1:]:
+    for g in near:
+        attend(per_half + g)
         away(g, QUERY)
     attend(0)
     wo_local.wait()
     for g in far:
-        forward(g)
         out_away(g)
     for g in near[1:]:
         attend(g)
     for g in near:
-        forward(g)
         oown[g] = terms(g)
+    writes = []
     for g in near:
         out_copy(g).wait_recv()
-        out_ref[rows_of(g), :] = (oown[g] + orecv[g].astype(F32)).astype(BF16)
+        oout[g] = (oown[g] + orecv[g].astype(F32)).astype(BF16)
+        writes.append(pltpu.make_async_copy(oout.at[g], out_ref.at[rows_of(g)], l_sem.at[g]))
+        writes[-1].start()
+    for copy in writes:
+        copy.wait()
 
     g_to_pair.wait_send()
     for copy in (*x_to_x, *x_to_pair, *x_forward, *w_pair.values()):
@@ -292,8 +296,8 @@
         vmem((held, out_width), BF16),
         vmem((pieces, chunk, 2 * width), BF16),
         vmem((pieces, chunk, 128), F32),
-        vmem((pieces, 8, chunk), F32),
-        vmem((pieces, 8, chunk), F32),
+        vmem((pieces, 1, chunk), F32),
+        vmem((pieces, 1, chunk), F32),
         vmem((pieces, chunk, 128), F32),
         vmem((pieces, 3, chunk, quarter), BF16),
         vmem((pieces, 3, chunk, quarter), BF16),
@@ -302,7 +306,8 @@
         vmem((pieces, chunk, held), BF16),
         vmem((per_half, chunk, out_width), BF16),
         vmem((per_half, chunk, out_width), BF16),
-        vmem((per_half, chunk, out_width), F32),
+        vmem((pieces, chunk, out_width), F32),
+        vmem((per_half, chunk, out_width), BF16),
         dma((8 + per_half,)),
         dma((1,)), dma((1,)),
         dma((3, per_half)), dma((3, per_half)),
@@ -315,11 +320,11 @@
     return pl.pallas_call(
         functools.partial(kernel, row_count, chunk),
         out_shape=jax.ShapeDtypeStruct((rows, out_width), BF16),
-        in_specs=[pl.BlockSpec(memory_space=pl.ANY)] * 6,
-        out_specs=pl.BlockSpec(memory_space=pltpu.VMEM),
+        in_specs=[pl.BlockSpec(memory_space=pltpu.HBM)] * 6,
+        out_specs=pl.BlockSpec(memory_space=pl.ANY),
         scratch_shapes=scratch,
         compiler_params=pltpu.CompilerParams(
-            collective_id=0, has_side_effects=True, vmem_limit_bytes=60 * 1024 * 1024),
+            collective_id=0, has_side_effects=True, vmem_limit_bytes=53 * 1024 * 1024),
     )(latents, norm_gain.reshape(1, width), k_weight, v_weight, q_weight, out_weight)
 
 

time: 61 us -> 60.8 us (level)
    unnamed x1 -> x3, local copies, waits for them, and re-layouts: 1.87 us -> 1.48 us
where the time goes in v3:
time: 60.8 us; the launch traced here: 60.6 us
  Pallas kernels  59.1 us (97%)
  local copies, waits for them, and re-layouts  1.48 us (2%)
    pallas_call x1, Pallas kernels, per_device(): pl.pallas_call(functools.partial(kernel, row_count, chunk), out_shape=jax...  59.1 us
    unnamed x3, local copies, waits for them, and re-layouts  1.48 us

profile of v3, /device:TPU:0, one launch (start us, length us, event | category | flops | bytes accessed | tf_op | source)
XLA Modules:
  0.0 60.6 jit_solution(15488382430398013812)
XLA Ops:
  0.0 0.0 copy-start
  0.0 0.7 %copy-done = f32[512]{0:T(512)S(1)} copy-done((f32[512]{0:T(512)S(1)}, f32[512]{0:T(512)}, u32[]{:S(2)}) %copy-start) | copy-done | bytes 2072
  0.7 59.1 %shard_map.64 = bf16[512,512]{1,0:T(8,128)(2,1)S(1)} custom-call(bf16[512,512]{1,0:T(8,128)(2,1)} %x_hbm.1, f32[1,512]{1,0:T(1,128)S(1)} %bitcast.1, bf16[512,1024]{1,0:T(8,128)(2,1)} %k_hbm.1, bf16[512,1024]{1,0:T(8,128)(2,1)} %v_hbm.1, bf16[512,1024]{1,0:T(8,128)(2,1)} %q_hbm.1, bf16[1024,512]{1,0:T(8,128)(2,1)} %o_hbm.1), custom_call_target="tpu_custom_call" | custom-call | tf_op jit(solution)/shard_map/pallas_call | solution.py:320
  59.8 0.8 %copy.8 = bf16[512,512]{1,0:T(8,128)(2,1)} copy(bf16[512,512]{1,0:T(8,128)(2,1)S(1)} %shard_map.64) | data formatting | bytes 1048576
Async XLA Ops:
  0.0 0.7 %copy-start = (f32[512]{0:T(512)S(1)}, f32[512]{0:T(512)}, u32[]{:S(2)}) copy-start(f32[512]{0:T(512)} %param.7) | copy-start | bytes 6148

commit v4 on v3

--- a/solution.py
+++ b/solution.py
@@ -194,21 +194,25 @@
         for t in (KEY, VALUE):
             combine(g, t)
 
-    def mixed_y(g):
-        block = mix.at[g, :, span(y, c)]
-        return remote(block, block, m_send.at[0, g], m_recv.at[0, g], ypeer)
-
-    def mixed_pair(g):
-        block = mix.at[g, :, span(y, c)]
-        return remote(block, block, m_send.at[1, g], m_recv.at[1, g], pair)
-
-    def mixed_forward(g):
-        block = mix.at[g, :, span(1 - y, c)]
-        return remote(block, block, m_send.at[2, g], m_recv.at[2, g], pair)
+    def head_of(y_at, h):
+        first = (2 * y_at + c) * quarter + h * HEAD_DIM
+        return pl.ds(pl.multiple_of(first, HEAD_DIM), HEAD_DIM)
+
+    def mixed_copy(kind, g, h, y_at, device):
+        block = mix.at[g, :, head_of(y_at, h)]
+        return remote(block, block, m_send.at[kind, g, h], m_recv.at[kind, g, h], device)
+
+    def mixed_y(g, h):
+        return mixed_copy(0, g, h, y, ypeer)
+
+    def mixed_pair(g, h):
+        return mixed_copy(1, g, h, y, pair)
+
+    def mixed_forward(g, h):
+        return mixed_copy(2, g, h, 1 - y, pair)
 
     def attend(g):
         combine(g, QUERY)
-        parts = []
         for h in range(heads_here):
             lanes = pl.ds(h * HEAD_DIM, HEAD_DIM)
             scores = lax.dot_general(
@@ -219,21 +223,22 @@
             denom = jnp.sum(weight, axis=1, keepdims=True)
             acc = jnp.dot(weight.astype(BF16), qkv[VALUE, :, lanes],
                           preferred_element_type=F32)
-            parts.append((acc / denom).astype(BF16))
-        mix[g, :, span(y, c)] = jnp.concatenate(parts, axis=1)
-        mixed_y(g).start()
-        mixed_pair(g).start()
+            mix[g, :, head_of(y, h)] = (acc / denom).astype(BF16)
+            mixed_y(g, h).start()
+            mixed_pair(g, h).start()
 
     def chip_terms(g, y_at):
         held = pl.ds(pl.multiple_of(2 * y_at * quarter, 2 * quarter), 2 * quarter)
         return jnp.dot(mix[g, :, held], wo[held, :], preferred_element_type=F32)
 
     def terms(g):
-        mixed_y(g).wait_recv()
-        mixed_forward(g).start()
-        mixed_pair(g).wait_recv()
+        for h in range(heads_here):
+            mixed_y(g, h).wait_recv()
+            mixed_forward(g, h).start()
+            mixed_pair(g, h).wait_recv()
         oown[g] = chip_terms(g, y)
-        mixed_forward(g).wait_recv()
+        for h in range(heads_here):
+            mixed_forward(g, h).wait_recv()
         return oown[g] + chip_terms(g, 1 - y)
 
     def out_copy(g):
@@ -246,11 +251,9 @@
     for g in near:
         attend(per_half + g)
         away(g, QUERY)
-    attend(0)
     wo_local.wait()
-    for g in far:
-        out_away(g)
-    for g in near[1:]:
+    for g in near:
+        out_away(per_half + g)
         attend(g)
     for g in near:
         oown[g] = terms(g)
@@ -270,9 +273,10 @@
         squares(g).wait_send()
         for t in range(3):
             partial(g, t).wait_send()
-        mixed_y(g).wait_send()
-        mixed_pair(g).wait_send()
-        mixed_forward(g).wait_send()
+        for h in range(heads_here):
+            mixed_y(g, h).wait_send()
+            mixed_pair(g, h).wait_send()
+            mixed_forward(g, h).wait_send()
     for g in near:
         out_copy(g).wait_send()
 
@@ -314,7 +318,7 @@
         dma((6,)), dma((6,)),
         dma((pieces,)), dma((pieces,)),
         dma((pieces, 3)), dma((pieces, 3)),
-        dma((3, pieces)), dma((3, pieces)),
+        dma((3, pieces, quarter // HEAD_DIM)), dma((3, pieces, quarter // HEAD_DIM)),
         dma((per_half,)), dma((per_half,)),
     ]
     return pl.pallas_call(
@@ -325,7 +329,7 @@
         scratch_shapes=scratch,
         compiler_params=pltpu.CompilerParams(
             collective_id=0, has_side_effects=True, vmem_limit_bytes=53 * 1024 * 1024),
-    )(latents, norm_gain.reshape(1, width), k_weight, v_weight, q_weight, out_weight)
+    )(latents, pltpu.with_memory_space_constraint(norm_gain.reshape(1, width), pltpu.HBM), k_weight, v_weight, q_weight, out_weight)
 
 
 def solution(mesh):

time: 60.8 us -> 56 us (0.921)
  Pallas kernels: 59.1 us -> 54.7 us
  local copies, waits for them, and re-layouts: 1.48 us -> 0.8 us
    pallas_call x1, Pallas kernels: 59.1 us -> 54.7 us  [per_device(): pl.pallas_call(functools.partial(kernel, row_count, chunk), out_shape=jax...]
    unnamed x3 -> x1, local copies, waits for them, and re-layouts: 1.48 us -> 0.8 us
where the time goes in v4:
time: 56 us; the launch traced here: 55.5 us
  Pallas kernels  54.7 us (98%)
  local copies, waits for them, and re-layouts  0.8 us (1%)
    pallas_call x1, Pallas kernels, per_device(): pl.pallas_call(functools.partial(kernel, row_count, chunk), out_shape=jax...  54.7 us

profile of v4, /device:TPU:0, one launch (start us, length us, event | category | flops | bytes accessed | tf_op | source)
XLA Modules:
  0.0 55.5 jit_solution(13058996441190329580)
XLA Ops:
  0.0 54.7 %shard_map.64 = bf16[512,512]{1,0:T(8,128)(2,1)S(1)} custom-call(bf16[512,512]{1,0:T(8,128)(2,1)} %x_hbm.1, f32[1,512]{1,0:T(1,128)} %bitcast.1, bf16[512,1024]{1,0:T(8,128)(2,1)} %k_hbm.1, bf16[512,1024]{1,0:T(8,128)(2,1)} %v_hbm.1, bf16[512,1024]{1,0:T(8,128)(2,1)} %q_hbm.1, bf16[1024,512]{1,0:T(8,128)(2,1)} %o_hbm.1), custom_call_target="tpu_custom_call" | custom-call | tf_op jit(solution)/shard_map/pallas_call | solution.py:324
  54.7 0.8 %copy.8 = bf16[512,512]{1,0:T(8,128)(2,1)} copy(bf16[512,512]{1,0:T(8,128)(2,1)S(1)} %shard_map.64) | data formatting | bytes 1048576

commit v5 on v4

--- a/solution.py
+++ b/solution.py
@@ -255,12 +255,11 @@
     for g in near:
         out_away(per_half + g)
         attend(g)
-    for g in near:
-        oown[g] = terms(g)
     writes = []
     for g in near:
+        total = terms(g)
         out_copy(g).wait_recv()
-        oout[g] = (oown[g] + orecv[g].astype(F32)).astype(BF16)
+        oout[g] = (total + orecv[g].astype(F32)).astype(BF16)
         writes.append(pltpu.make_async_copy(oout.at[g], out_ref.at[rows_of(g)], l_sem.at[g]))
         writes[-1].start()
     for copy in writes:

time: 56 us -> 55.9 us (level)
  no operation moved by 1% of the time
where the time goes in v5:
time: 55.9 us; the launch traced here: 55.5 us
  Pallas kernels  54.7 us (98%)
  local copies, waits for them, and re-layouts  0.8 us (1%)
    pallas_call x1, Pallas kernels, per_device(): pl.pallas_call(functools.partial(kernel, row_count, chunk), out_shape=jax...  54.7 us

profile of v5, /device:TPU:0, one launch (start us, length us, event | category | flops | bytes accessed | tf_op | source)
XLA Modules:
  0.0 55.5 jit_solution(14379679446437940394)
XLA Ops:
  0.0 54.7 %shard_map.64 = bf16[512,512]{1,0:T(8,128)(2,1)S(1)} custom-call(bf16[512,512]{1,0:T(8,128)(2,1)} %x_hbm.1, f32[1,512]{1,0:T(1,128)} %bitcast.1, bf16[512,1024]{1,0:T(8,128)(2,1)} %k_hbm.1, bf16[512,1024]{1,0:T(8,128)(2,1)} %v_hbm.1, bf16[512,1024]{1,0:T(8,128)(2,1)} %q_hbm.1, bf16[1024,512]{1,0:T(8,128)(2,1)} %o_hbm.1), custom_call_target="tpu_custom_call" | custom-call | tf_op jit(solution)/shard_map/pallas_call | solution.py:323
  54.7 0.8 %copy.8 = bf16[512,512]{1,0:T(8,128)(2,1)} copy(bf16[512,512]{1,0:T(8,128)(2,1)S(1)} %shard_map.64) | data formatting | bytes 1048576
